TPU v7x, 32 devices: a whole 2x2x4 slice. The times are simulated.
32 devices in a mesh: src: 4 (over y, core), help: 8 (over z, x).
Axes of the slice: x: 2, y: 2, z: 4, core: 2. Of those that a mesh axis runs over, the one named last changes fastest.
Arguments:
- tiles: int32 [2, 256], P(None, 'src'), may hold values from 0 to 31, as said below
- cell_slot: int32 [2, 32], replicated, may hold values from 0 to 31, as said below
- counts: int32 [32, 2], P(('src', 'help')), may hold values from 128 to 512, as said below
- src_points: bfloat16 [16384, 512], P(('src', 'help')), may hold values from -9 to 9
- tgt_points: bfloat16 [16384, 512], P(('src', 'help')), may hold values from -9 to 9
Outputs:
- source_potential: float32 [16384], P(('src', 'help'))
- target_potential: float32 [16384], P(('src', 'help'))
- transport: float32 [16384, 512], P(('src', 'help'))
Inputs may be any that keep to these rules, and one draw needn't show every extreme that they name: `tiles`: columns come in blocks of 64, block g for group g of 8 cells: a block's source cells have ids g * 8 to g * 8 + 7, its target cells lie in group g or in group g + 1 (group 4 - 1 is followed by group 0); no pair is listed twice, and every source cell and every target cell is named in some column. Each row is a permutation that keeps every cell in its group: cell c is stored at slot cell_slot[side, c], with cell_slot[side, c] // 8 equal to c // 8; slot k is rows k * 512 to k * 512 + 511 of the point arrays. `counts`: rows of a slot at and beyond its count are padding. Both ends of the range occur in each column.
All inputs are finite; a program needn't handle non-finite values.
Results may differ from a plain program's by a relative error of at most 0.004.
Values may be sent and summed in bfloat16 or wider, within the bound.
A program may use at most 192 MiB of HBM per device.

v0:
```python
import math
import jax
import jax.numpy as jnp
from jax import lax
from jax.sharding import PartitionSpec as P

ITERS = 2
EPSILON = 0.2
NEGATIVE = -1e30


def passed_along(array, axis, by):
    count = lax.axis_size(axis)
    return lax.ppermute(array, axis, [(i, (i + by) % count) for i in range(count)])


def combined_all(part, axis, combine):
    gathered = jax.tree.map(lambda a: lax.all_gather(a, axis), part)

    def take(source):
        return jax.tree.map(lambda a: lax.dynamic_index_in_dim(a, source, 0, False), gathered)

    return lax.fori_loop(
        1, lax.axis_size(axis), lambda source, state: combine(state, take(source)), take(0)
    )


def join_parts(first, second):
    highest = jnp.maximum(first[0], second[0])
    return (
        highest,
        first[1] * jnp.exp(first[0] - highest) + second[1] * jnp.exp(second[0] - highest),
    )


def lookup(cell_ids, slot_table):
    matches = cell_ids[:, None] == jnp.arange(slot_table.shape[0], dtype=jnp.int32)[None, :]
    return jnp.sum(jnp.where(matches, slot_table[None, :], 0), axis=1)


def half_norms(points, group_size, cell_rows):
    return 0.5 * jnp.sum(jnp.square(points.astype(jnp.float32)), axis=1).reshape(
        group_size, cell_rows
    )


def shards(tiles, cell_slot, counts, src_points, tgt_points):
    group_size = lax.axis_size("help")
    help_index = lax.axis_index("help")
    src_index = lax.axis_index("src")
    cell_rows = src_points.shape[0]
    width = src_points.shape[1]
    cost_scale = math.sqrt(width)
    source_all, source_counts = (src_points, counts)
    source_cells_held = 1
    own_points, own_counts = (
        lax.all_gather(tgt_points, "help", axis=0, tiled=True),
        lax.all_gather(counts, "help", axis=0, tiled=True),
    )
    next_points, next_counts = passed_along((own_points, own_counts), "src", -1)
    candidates = 2 * group_size
    positions = jnp.arange(cell_rows, dtype=jnp.int32)
    source_live = positions[None, :] < source_counts[:, 0:1]
    target_live = jnp.stack(
        [positions[None, :] < own_counts[:, 1:2], positions[None, :] < next_counts[:, 1:2]], axis=0
    )
    flat_live = target_live.reshape(candidates, cell_rows)
    source_half = half_norms(source_all, source_cells_held, cell_rows)
    target_half = jnp.stack(
        [
            half_norms(own_points, group_size, cell_rows),
            half_norms(next_points, group_size, cell_rows),
        ],
        axis=0,
    )
    flat_half = target_half.reshape(candidates, cell_rows)
    target_points = jnp.concatenate([own_points, next_points], axis=0)
    src_slot = lookup(tiles[0], cell_slot[0])
    tgt_slot = lookup(tiles[1], cell_slot[1])
    src_cells = src_slot % group_size
    tgt_cells = tgt_slot % group_size
    tgt_sides = jnp.where(tgt_slot // group_size == src_index, 0, 1)
    tgt_keys = tgt_sides * group_size + tgt_cells
    key_ids = jnp.arange(candidates, dtype=jnp.int32)
    is_mine = src_cells == help_index
    listed_keys = jnp.any(is_mine[:, None] & (tgt_keys[:, None] == key_ids[None, :]), axis=0)
    inner = lax.dot_general(
        src_points, target_points, (((1,), (1,)), ((), ())), preferred_element_type=jnp.float32
    )
    cost = (source_half[0][:, None] + flat_half.reshape(-1)[None, :] - inner) / cost_scale
    column_live = (flat_live & listed_keys[:, None]).reshape(-1)
    mask = source_live[0][:, None] & column_live[None, :]
    own_live = source_live[0]
    target_table = jnp.zeros((2, group_size, cell_rows), jnp.float32)
    source_table = jnp.zeros((source_cells_held, cell_rows), jnp.float32)
    source_own = jnp.zeros((cell_rows,), jnp.float32)
    target_own = jnp.zeros((cell_rows,), jnp.float32)
    for sweep in range(ITERS):
        row_flat_target = target_table.reshape(candidates, cell_rows)
        row_scores = jnp.where(
            mask, (row_flat_target.reshape(-1)[None, :] - cost) / EPSILON, NEGATIVE
        )
        part_max = jnp.max(row_scores, axis=1)
        part_sum = jnp.sum(jnp.exp(row_scores - part_max[:, None]), axis=1)
        row_source_own = jnp.where(own_live, -EPSILON * (part_max + jnp.log(part_sum)), 0.0)
        row_source_table = row_source_own[None, :]
        source_table = row_source_table
        source_own = row_source_own
        scores = jnp.where(mask, (source_table[0][:, None] - cost) / EPSILON, NEGATIVE)
        peaks = jnp.max(scores, axis=0)
        sums = jnp.sum(jnp.exp(scores - peaks[None, :]), axis=0)
        peaks = peaks.reshape(2, group_size, cell_rows)
        sums = sums.reshape(2, group_size, cell_rows)
        peaks, sums = combined_all((peaks, sums), "help", join_parts)
        carried_max, carried_sum = passed_along((peaks[1], sums[1]), "src", 1)
        joined = join_parts((peaks[0], sums[0]), (carried_max, carried_sum))
        target_group = jnp.where(target_live[0], -EPSILON * (joined[0] + jnp.log(joined[1])), 0.0)
        target_after = passed_along(target_group, "src", -1)
        col_target_table = jnp.stack([target_group, target_after], axis=0)
        col_target_own = target_group[help_index]
        target_table = col_target_table
        target_own = col_target_own
    flat_target = target_table.reshape(candidates, cell_rows)
    exponent = (source_table[0][:, None] + flat_target.reshape(-1)[None, :] - cost) / EPSILON
    weight = jnp.where(mask, jnp.exp(exponent), 0.0).astype(jnp.bfloat16)
    own_numerator = jnp.dot(weight, target_points, preferred_element_type=jnp.float32)
    own_denominator = jnp.sum(weight.astype(jnp.float32), axis=1)
    safe_total = jnp.where(own_live, own_denominator, 1.0)
    transport = jnp.where(own_live[:, None], own_numerator / safe_total[:, None], 0.0)
    return (source_own, target_own, transport)


def solution(mesh):
    in_specs = (
        P(None, "src"),
        P(),
        P(("src", "help"), None),
        P(("src", "help"), None),
        P(("src", "help"), None),
    )
    out_specs = (P(("src", "help")), P(("src", "help")), P(("src", "help"), None))
    return jax.shard_map(shards, mesh=mesh, in_specs=in_specs, out_specs=out_specs, check_vma=False)
```

profile of v0, /device:TPU:1, one launch (start us, length us, event | category | flops | bytes accessed | tf_op | source)
XLA Modules:
  0.0 362.8 jit_solution(11354192799630096327)
XLA Ops:
  7.2 0.7 all-gather.3.cloned.1.call-update
  7.9 75.9 %all-gather.3.cloned.1.call-done = bf16[4096,512]{1,0:T(8,128)(2,1)} async-done(((bf16[512,512]{1,0:T(8,128)(2,1)}), bf16[4096,512]{1,0:T(8,128)(2,1)}) %all-gather.3.cloned.1.call-update) | async-done | bytes 4194320 | tf_op jit(solution)/shard_map/all_gather | solution.py:57
  83.8 1.9 collective-permute-start.1
  85.7 14.5 %all-gather = s32[8,1,2]{2,1,0:T(1,128)S(1)} all-gather(s32[1,1,2]{2,1,0:T(1,128)} %bitcast.156), channel_id=1, replica_groups=mesh['src'=4,'help'=8] {'help'}, dimensions={0}, use_global_device_ids=true | all-gather | bytes 72 | tf_op jit(solution)/shard_map/all_gather | solution.py:58
  100.2 0.1 copy.10
  100.3 4.6 %collective-permute-start = (s32[8,2]{0,1:T(2,128)S(1)}, s32[8,2]{0,1:T(2,128)S(1)}, u32[]{:S(2)}, u32[]{:S(2)}) collective-permute-start(s32[8,2]{0,1:T(2,128)S(1)} %bitcast.162), channel_id=1, source_target_pairs={{0,24},{8,0},{16,8},{24,16},{1,25},{9,1},{17,9},{25,17},{2,26},{10... | collective-permute-start | bytes 200 | tf_op jit(solution)/shard_map/ppermute | solution.py:14
  104.8 0.6 iota_compare_fusion.6
  105.5 0.8 slice_bitcast_fusion.11
  106.3 0.8 slice_bitcast_fusion.10
  107.0 0.1 select_reduce_fusion
  107.1 0.1 fusion.30
  107.3 1.2 multiply_reduce_fusion.2
  108.5 0.1 iota_compare_fusion.4
  108.6 0.1 broadcast_bitcast_fusion
  108.7 24.6 %collective-permute-done = s32[8,2]{0,1:T(2,128)S(1)} collective-permute-done((s32[8,2]{0,1:T(2,128)S(1)}, s32[8,2]{0,1:T(2,128)S(1)}, u32[]{:S(2)}, u32[]{:S(2)}) %collective-permute-start) | collective-permute-done | bytes 96 | tf_op jit(solution)/shard_map/ppermute | solution.py:14
  133.3 0.1 iota_compare_fusion.3
  133.4 3.1 multiply_reduce_fusion.1
  136.5 4.4 %constant_dynamic-update-slice_fusion.1 = bf16[8192,512]{1,0:T(8,128)(2,1)} fusion(bf16[4096,512]{1,0:T(8,128)(2,1)} %all-gather.3.cloned.1.call-done), kind=kLoop, calls=%fused_computation.82 | loop fusion | bytes 8388608
  140.9 3.1 multiply_reduce_fusion
  144.0 4.4 %constant_dynamic-update-slice_fusion = bf16[8192,512]{1,0:T(8,128)(2,1)} fusion(bf16[8192,512]{1,0:T(8,128)(2,1)} %constant_dynamic-update-slice_fusion.1, bf16[4096,512]{1,0:T(8,128)(2,1)} %collective-permute-done.1), kind=kLoop, calls=%fused_computation.81 | loop fusion | bytes 8388608 | tf_op jit(solution)/shard_map/concatenate | solution.py:77
  148.4 10.4 %fusion.6 = (f32[512]{0:T(512)S(1)}, f32[512,8192]{0,1:T(8,128)S(1)}) fusion(pred[512]{0:T(512)(128)(4,1)S(1)} %iota_compare_fusion.6, pred[8192]{0:T(1024)(128)(4,1)S(1)} %and.81, bf16[8192,512]{1,0:T(8,128)(2,1)} %constant_dynamic-update-slice_fusion, bf16[512,512]{1,0:T(8,128)(2,1)S(1)} %copy-done.2, f32[8192]{0:T(1024)S(1)} %bitcast.153, ...), kind=kOutput, calls=%fused_computation.23 | convolution fusion | flops 4328521216 | bytes 25735680 | tf_op jit(solution)/shard_map/dot_general | solution.py:87
  158.9 7.0 %exponential_reduce_fusion.3 = f32[512]{0:T(512)S(1)} fusion(f32[512,8192]{0,1:T(8,128)S(1)} %get-tuple-element.304, f32[512]{0:T(512)S(1)} %get-tuple-element.303, pred[512]{0:T(512)(128)(4,1)S(1)} %iota_compare_fusion.6, pred[8192]{0:T(1024)(128)(4,1)S(1)} %and.81), kind=kLoop, calls=%fused_computation.22 | loop fusion | flops 25165312 | bytes 16790016 | tf_op jit(solution)/shard_map/reduce_sum | solution.py:104
  166.0 4.8 %fusion.7 = f32[8192]{0:T(1024)S(1)} fusion(f32[512,8192]{0,1:T(8,128)S(1)} %get-tuple-element.304, f32[512]{0:T(512)S(1)} %multiply_select_fusion.1, pred[512]{0:T(512)(128)(4,1)S(1)} %iota_compare_fusion.6, pred[8192]{0:T(1024)(128)(4,1)S(1)} %and.81), kind=kLoop, calls=%fused_computation.24 | loop fusion | flops 20963328 | bytes 16820736 | tf_op jit(solution)/shard_map/reduce_max | solution.py:110
  170.8 6.7 %exponential_reduce_fusion.2 = f32[8192]{0:T(1024)S(1)} fusion(f32[512,8192]{0,1:T(8,128)S(1)} %get-tuple-element.304, f32[8192]{0:T(1024)S(1)} %fusion.7, f32[512]{0:T(512)S(1)} %multiply_select_fusion.1, pred[512]{0:T(512)(128)(4,1)S(1)} %iota_compare_fusion.6, pred[8192]{0:T(1024)(128)(4,1)S(1)} %and.81), kind=kLoop, calls=%fused_computation.21 | loop fusion | flops 25157632 | bytes 16853504 | tf_op jit(solution)/shard_map/reduce_sum | solution.py:111
  177.5 24.8 %all_gather.21 = f32[8,2,8,512]{3,2,1,0:T(8,128)S(1)} all-gather(f32[1,2,8,512]{3,2,1,0:T(8,128)S(1)} %all_gather_reshape.13), channel_id=1, replica_groups=mesh['src'=4,'help'=8] {'help'}, dimensions={0}, use_global_device_ids=true | all-gather | bytes 294912 | tf_op jit(solution)/shard_map/all_gather | solution.py:18
  202.4 24.9 %all_gather.20 = f32[8,2,8,512]{3,2,1,0:T(8,128)S(1)} all-gather(f32[1,2,8,512]{3,2,1,0:T(8,128)S(1)} %all_gather_reshape.12), channel_id=1, replica_groups=mesh['src'=4,'help'=8] {'help'}, dimensions={0}, use_global_device_ids=true | all-gather | bytes 294912 | tf_op jit(solution)/shard_map/all_gather | solution.py:18
  227.3 0.4 while.34
  227.7 11.7 %collective-permute-start.2 = (f32[8,512]{1,0:T(8,128)S(1)}, f32[8,512]{1,0:T(8,128)S(1)}, u32[]{:S(2)}, u32[]{:S(2)}) collective-permute-start(f32[8,512]{1,0:T(8,128)S(1)} %slice_bitcast_fusion.7), channel_id=1, source_target_pairs={{0,8},{8,16},{16,24},{24,0},{1,9},{9,17},{17,25},{25,1},{2,10},{10... | collective-permute-start | bytes 49160 | tf_op jit(solution)/shard_map/ppermute | solution.py:14
  239.5 0.8 collective-permute-done.2
  240.3 0.3 collective-permute-done.3
  240.6 0.1 fusion.24
  240.7 1.3 collective-permute-start.4
  242.0 2.3 collective-permute-done.4
  244.3 10.3 %fusion.8 = f32[512]{0:T(512)S(1)} fusion(f32[512,8192]{0,1:T(8,128)} %copy-done, f32[8192]{0:T(1024)S(1)} %bitcast.146, pred[512]{0:T(512)(128)(4,1)S(1)} %iota_compare_fusion.6, pred[8192]{0:T(1024)(128)(4,1)S(1)} %and.81), kind=kLoop, calls=%fused_computation.25 | loop fusion | flops 20971008 | bytes 16820736 | tf_op jit(solution)/shard_map/reduce_max | solution.py:103
  254.6 5.6 %exponential_reduce_fusion.1 = f32[512]{0:T(512)S(1)} fusion(f32[512,8192]{0,1:T(8,128)S(1)} %copy-done.1, f32[512]{0:T(512)S(1)} %fusion.8, f32[8192]{0:T(1024)S(1)} %bitcast.147, pred[512]{0:T(512)(128)(4,1)S(1)} %iota_compare_fusion.6, pred[8192]{0:T(1024)(128)(4,1)S(1)} %and.81), kind=kLoop, calls=%fused_computation.20 | loop fusion | flops 25165312 | bytes 16822784 | tf_op jit(solution)/shard_map/reduce_sum | solution.py:104
  260.2 4.8 %fusion.9 = f32[8192]{0:T(1024)S(1)} fusion(f32[512,8192]{0,1:T(8,128)S(1)} %copy-done.1, f32[512]{0:T(512)S(1)} %multiply_select_fusion, pred[512]{0:T(512)(128)(4,1)S(1)} %iota_compare_fusion.6, pred[8192]{0:T(1024)(128)(4,1)S(1)} %and.81), kind=kLoop, calls=%fused_computation.26 | loop fusion | flops 20963328 | bytes 16820736 | tf_op jit(solution)/shard_map/reduce_max | solution.py:110
  265.1 6.7 %exponential_reduce_fusion = f32[8192]{0:T(1024)S(1)} fusion(f32[512,8192]{0,1:T(8,128)S(1)} %copy-done.1, f32[8192]{0:T(1024)S(1)} %fusion.9, f32[512]{0:T(512)S(1)} %multiply_select_fusion, pred[512]{0:T(512)(128)(4,1)S(1)} %iota_compare_fusion.6, pred[8192]{0:T(1024)(128)(4,1)S(1)} %and.81), kind=kLoop, calls=%fused_computation.19 | loop fusion | flops 25157632 | bytes 16853504 | tf_op jit(solution)/shard_map/reduce_sum | solution.py:111
  271.8 25.1 %all_gather.23 = f32[8,2,8,512]{3,2,1,0:T(8,128)S(1)} all-gather(f32[1,2,8,512]{3,2,1,0:T(8,128)S(1)} %all_gather_reshape.15), channel_id=1, replica_groups=mesh['src'=4,'help'=8] {'help'}, dimensions={0}, use_global_device_ids=true | all-gather | bytes 294912 | tf_op jit(solution)/shard_map/all_gather | solution.py:18
  296.9 24.9 %all_gather.22 = f32[8,2,8,512]{3,2,1,0:T(8,128)S(1)} all-gather(f32[1,2,8,512]{3,2,1,0:T(8,128)S(1)} %all_gather_reshape.14), channel_id=1, replica_groups=mesh['src'=4,'help'=8] {'help'}, dimensions={0}, use_global_device_ids=true | all-gather | bytes 294912 | tf_op jit(solution)/shard_map/all_gather | solution.py:18
  321.8 0.4 while.35
  322.2 11.8 %collective-permute-start.5 = (f32[8,512]{1,0:T(8,128)S(1)}, f32[8,512]{1,0:T(8,128)S(1)}, u32[]{:S(2)}, u32[]{:S(2)}) collective-permute-start(f32[8,512]{1,0:T(8,128)S(1)} %slice_bitcast_fusion.5), channel_id=1, source_target_pairs={{0,8},{8,16},{16,24},{24,0},{1,9},{9,17},{17,25},{25,1},{2,10},{10... | collective-permute-start | bytes 49160 | tf_op jit(solution)/shard_map/ppermute | solution.py:14
  334.1 0.8 collective-permute-done.5
  334.9 0.3 collective-permute-done.6
  335.3 1.4 collective-permute-start.7
  336.7 0.6 constant_dynamic-slice_fusion
  337.3 1.6 collective-permute-done.7
  338.9 8.1 %convert_reduce_fusion = (f32[512]{0:T(512)S(1)}, bf16[512,8192]{0,1:T(8,128)(2,1)S(1)}) fusion(f32[512,8192]{0,1:T(8,128)} %copy-done, f32[8192]{0:T(1024)S(1)} %bitcast.148, f32[512]{0:T(512)S(1)} %multiply_select_fusion, pred[8192]{0:T(1024)(128)(4,1)S(1)} %and.81, pred[512]{0:T(512)(128)(4,1)S(1)} %iota_compare_fusion.6), kind=kLoop, calls=%fused_computation.18 | loop fusion | flops 33553920 | bytes 25211392 | tf_op jit(solution)/shard_map/reduce_sum | solution.py:127
  347.1 8.9 %fusion.10 = f32[512,512]{1,0:T(8,128)} fusion(bf16[512,8192]{0,1:T(8,128)(2,1)S(1)} %get-tuple-element.298, bf16[8192,512]{1,0:T(8,128)(2,1)} %constant_dynamic-update-slice_fusion, f32[512]{0:T(512)S(1)} %broadcast_select_fusion, pred[512]{0:T(512)(128)(4,1)S(1)} %iota_compare_fusion.6), kind=kOutput, calls=%fused_computation.30 | convolution fusion | flops 4295491584 | bytes 17828352 | tf_op jit(solution)/shard_map/dot_general | solution.py:126
  (63 shorter events, 1.0 us)
Async XLA Ops:
  7.2 141.3 %copy-start.2 = (bf16[512,512]{1,0:T(8,128)(2,1)S(1)}, bf16[512,512]{1,0:T(8,128)(2,1)}, u32[]{:S(2)}) copy-start(bf16[512,512]{1,0:T(8,128)(2,1)} %param.12) | copy-start | bytes 1572868
  7.2 76.6 %all-gather.3.cloned.1.call-start = ((), (), s32[]{:S(2)}) async-start(), calls=%async_computation | async-start | bytes 4718592 | tf_op jit(solution)/shard_map/all_gather | solution.py:57
  83.8 57.1 %collective-permute-start.1 = (bf16[4096,512]{1,0:T(8,128)(2,1)}, bf16[4096,512]{1,0:T(8,128)(2,1)}, u32[]{:S(2)}, u32[]{:S(2)}) collective-permute-start(bf16[4096,512]{1,0:T(8,128)(2,1)} %all-gather.3.cloned.1.call-done), channel_id=1, source_target_pairs={{0,24},{8,0},{16,8},{24,16},{1,25},{9,1},{17,9},{25,17},{2,26},{10... | collective-permute-start | bytes 12582920 | tf_op jit(solution)/shard_map/ppermute | solution.py:14
  100.3 33.0 %collective-permute-start = (s32[8,2]{0,1:T(2,128)S(1)}, s32[8,2]{0,1:T(2,128)S(1)}, u32[]{:S(2)}, u32[]{:S(2)}) collective-permute-start(s32[8,2]{0,1:T(2,128)S(1)} %bitcast.162), channel_id=1, source_target_pairs={{0,24},{8,0},{16,8},{24,16},{1,25},{9,1},{17,9},{25,17},{2,26},{10... | collective-permute-start | bytes 200 | tf_op jit(solution)/shard_map/ppermute | solution.py:14
  158.9 11.9 %copy-start = (f32[512,8192]{0,1:T(8,128)}, f32[512,8192]{0,1:T(8,128)S(1)}, u32[]{:S(2)}) copy-start(f32[512,8192]{0,1:T(8,128)S(1)} %get-tuple-element.304) | copy-start | bytes 50331652
  158.9 7.0 %copy-start.4 = (s32[1,2]{1,0:T(1,128)S(1)}, s32[1,2]{1,0:T(1,128)}, u32[]{:S(2)}) copy-start(s32[1,2]{1,0:T(1,128)} %param.11) | copy-start | bytes 28
  227.7 12.6 %collective-permute-start.2 = (f32[8,512]{1,0:T(8,128)S(1)}, f32[8,512]{1,0:T(8,128)S(1)}, u32[]{:S(2)}, u32[]{:S(2)}) collective-permute-start(f32[8,512]{1,0:T(8,128)S(1)} %slice_bitcast_fusion.7), channel_id=1, source_target_pairs={{0,8},{8,16},{16,24},{24,0},{1,9},{9,17},{17,25},{25,1},{2,10},{10... | collective-permute-start | bytes 49160 | tf_op jit(solution)/shard_map/ppermute | solution.py:14
  239.4 1.2 collective-permute-start.3
  240.7 3.6 collective-permute-start.4
  242.0 12.6 %copy-start.1 = (f32[512,8192]{0,1:T(8,128)S(1)}, f32[512,8192]{0,1:T(8,128)}, u32[]{:S(2)}) copy-start(f32[512,8192]{0,1:T(8,128)} %copy-done) | copy-start | bytes 50331652
  260.2 78.7 %copy-start.3 = (f32[512]{0:T(512)}, f32[512]{0:T(512)S(1)}, u32[]{:S(2)}) copy-start(f32[512]{0:T(512)S(1)} %multiply_select_fusion) | copy-start | bytes 6148
  322.2 12.7 %collective-permute-start.5 = (f32[8,512]{1,0:T(8,128)S(1)}, f32[8,512]{1,0:T(8,128)S(1)}, u32[]{:S(2)}, u32[]{:S(2)}) collective-permute-start(f32[8,512]{1,0:T(8,128)S(1)} %slice_bitcast_fusion.5), channel_id=1, source_target_pairs={{0,8},{8,16},{16,24},{24,0},{1,9},{9,17},{17,25},{25,1},{2,10},{10... | collective-permute-start | bytes 49160 | tf_op jit(solution)/shard_map/ppermute | solution.py:14
  334.1 1.2 collective-permute-start.6
  335.3 3.6 collective-permute-start.7
Sparse Core Ops, SparseCore 0:
  10.1 73.6 all-gather.2
where the time goes:
time: 363 us
  blocking collectives  114 us (31%)
  waiting for transfers between devices  107 us (29%)
  other arithmetic  63.1 us (17%)
  starting transfers between devices  32.9 us (9%)
  matrix products  19.3 us (5%)
  between operations  14.4 us (4%)
  local copies, waits for them, and re-layouts  11.2 us (3%)
    all_gather x4, blocking collectives, combined_all(): gathered = jax.tree.map(lambda a: lax.all_gather(a, axis), part)  99.8 us
    all_gather x1, waiting for transfers between devices, shards(): lax.all_gather(tgt_points, 'help', axis=0, tiled=True)  75.9 us
    ppermute x8, starting transfers between devices, passed_along(): lax.ppermute(array, axis, [(i, (i + by) % count) for i in range(count)])  32.8 us
    ppermute x8, waiting for transfers between devices, passed_along(): lax.ppermute(array, axis, [(i, (i + by) % count) for i in range(count)])  30.7 us
    all_gather x1, blocking collectives, shards(): lax.all_gather(counts, 'help', axis=0, tiled=True)  14.5 us
    reduce_sum x2, other arithmetic, shards(): sums = jnp.sum(jnp.exp(scores - peaks[None, :]), axis=0)  13.3 us
    reduce_sum x2, other arithmetic, shards(): part_sum = jnp.sum(jnp.exp(row_scores - part_max[:, None]), axis=1)  12.6 us
    dot_general x1, matrix products, shards(): lax.dot_general(src_points, target_points, (((1,), (1,)), ((), ())), pref...  10.4 us
  transfers between devices with their start and end apart: 9, of which 8 were waited for; matrix products, arithmetic and copies ran while one was open for 3% of the time, Pallas kernels for 0%

commit v1 on v0

--- a/solution.py
+++ b/solution.py
@@ -7,6 +7,23 @@
 ITERS = 2
 EPSILON = 0.2
 NEGATIVE = -1e30
+
+
+def joined_along(blocks, dim):
+    blocks = jnp.moveaxis(blocks, 0, dim)
+    lengths = blocks.shape
+    return blocks.reshape(*lengths[:dim], lengths[dim] * lengths[dim + 1], *lengths[dim + 2 :])
+
+
+def ring_gather(value, axis, dim):
+    length = lax.axis_size(axis)
+    ahead = [(i, (i + 1) % length) for i in range(length)]
+    blocks = [value]
+    while len(blocks) < length:
+        blocks.append(lax.ppermute(blocks[-1], axis, ahead))
+    index = lax.axis_index(axis)
+    blocks = jnp.stack(blocks)[(index - jnp.arange(length)) % length]
+    return joined_along(blocks, dim)
 
 
 def passed_along(array, axis, by):
@@ -54,7 +71,7 @@
     source_all, source_counts = (src_points, counts)
     source_cells_held = 1
     own_points, own_counts = (
-        lax.all_gather(tgt_points, "help", axis=0, tiled=True),
+        ring_gather(tgt_points, "help", 0),
         lax.all_gather(counts, "help", axis=0, tiled=True),
     )
     next_points, next_counts = passed_along((own_points, own_counts), "src", -1)

time: 363 us -> 369 us (1.017)
  between operations: 14.4 us -> 1.04 us
  waiting for transfers between devices: 107 us -> 119 us
  starting transfers between devices: 32.9 us -> 41.4 us
    ppermute x0 -> x7, waiting for transfers between devices: none -> 84.7 us  [ring_gather(): blocks.append(lax.ppermute(blocks[-1], axis, ahead))]
    all_gather x1 -> x0, waiting for transfers between devices: 75.9 us -> none  [shards(): lax.all_gather(tgt_points, 'help', axis=0, tiled=True)]
    ppermute x8, starting transfers between devices: 32.8 us -> 39.3 us  [passed_along(): lax.ppermute(array, axis, [(i, (i + by) % count) for i in range(count)])]
    gather x0 -> x1, local copies, waits for them, and re-layouts: none -> 4.92 us  [ring_gather(): blocks = jnp.stack(blocks)[(index - jnp.arange(length)) % length]]
    concatenate x1 -> x0, local copies, waits for them, and re-layouts: 4.43 us -> none  [shards(): target_points = jnp.concatenate([own_points, next_points], axis=0)]
  transfers between devices with their start and end apart: 9 -> 15, of which waited for: 8 -> 14; matrix products, arithmetic and copies ran while one was open for 3% -> 3% of each run, Pallas kernels for 0% -> 0%
where the time goes in v1:
time: 369 us
  waiting for transfers between devices  119 us (32%)
  blocking collectives  111 us (30%)
  other arithmetic  61.3 us (17%)
  starting transfers between devices  41.4 us (11%)
  matrix products  20.8 us (6%)
  local copies, waits for them, and re-layouts  13.6 us (4%)
    all_gather x4, blocking collectives, combined_all(): gathered = jax.tree.map(lambda a: lax.all_gather(a, axis), part)  98.5 us
    ppermute x7, waiting for transfers between devices, ring_gather(): blocks.append(lax.ppermute(blocks[-1], axis, ahead))  84.7 us
    ppermute x8, starting transfers between devices, passed_along(): lax.ppermute(array, axis, [(i, (i + by) % count) for i in range(count)])  39.3 us
    ppermute x8, waiting for transfers between devices, passed_along(): lax.ppermute(array, axis, [(i, (i + by) % count) for i in range(count)])  34.2 us
    reduce_sum x2, other arithmetic, shards(): sums = jnp.sum(jnp.exp(scores - peaks[None, :]), axis=0)  13.3 us
    dot_general x1, matrix products, shards(): lax.dot_general(src_points, target_points, (((1,), (1,)), ((), ())), pref...  13.1 us
    all_gather x1, blocking collectives, shards(): lax.all_gather(counts, 'help', axis=0, tiled=True)  12.8 us
    reduce_sum x2, other arithmetic, shards(): part_sum = jnp.sum(jnp.exp(row_scores - part_max[:, None]), axis=1)  12.6 us
  transfers between devices with their start and end apart: 15, of which 14 were waited for; matrix products, arithmetic and copies ran while one was open for 3% of the time, Pallas kernels for 0%

profile of v1, /device:TPU:1, one launch (start us, length us, event | category | flops | bytes accessed | tf_op | source)
XLA Modules:
  0.0 368.6 jit_solution(17810984941617853211)
XLA Ops:
  0.7 2.1 collective-permute-start.1
  2.8 14.9 %collective-permute-done.1 = bf16[512,512]{1,0:T(8,128)(2,1)S(1)} collective-permute-done((bf16[512,512]{1,0:T(8,128)(2,1)}, bf16[512,512]{1,0:T(8,128)(2,1)S(1)}, u32[]{:S(2)}, u32[]{:S(2)}) %collective-permute-start.1) | collective-permute-done | bytes 524320 | tf_op jit(solution)/shard_map/ppermute | solution.py:23
  17.6 14.9 %collective-permute-done.2 = bf16[512,512]{1,0:T(8,128)(2,1)S(1)} collective-permute-done((bf16[512,512]{1,0:T(8,128)(2,1)S(1)}, bf16[512,512]{1,0:T(8,128)(2,1)S(1)}, u32[]{:S(2)}, u32[]{:S(2)}) %collective-permute-start.2) | collective-permute-done | bytes 524320 | tf_op jit(solution)/shard_map/ppermute | solution.py:23
  32.6 14.1 %collective-permute-done.3 = bf16[512,512]{1,0:T(8,128)(2,1)S(1)} collective-permute-done((bf16[512,512]{1,0:T(8,128)(2,1)S(1)}, bf16[512,512]{1,0:T(8,128)(2,1)S(1)}, u32[]{:S(2)}, u32[]{:S(2)}) %collective-permute-start.3) | collective-permute-done | bytes 524320 | tf_op jit(solution)/shard_map/ppermute | solution.py:23
  46.6 13.2 %collective-permute-done.4 = bf16[512,512]{1,0:T(8,128)(2,1)S(1)} collective-permute-done((bf16[512,512]{1,0:T(8,128)(2,1)S(1)}, bf16[512,512]{1,0:T(8,128)(2,1)S(1)}, u32[]{:S(2)}, u32[]{:S(2)}) %collective-permute-start.4) | collective-permute-done | bytes 524320 | tf_op jit(solution)/shard_map/ppermute | solution.py:23
  59.9 1.9 bitcast_dynamic-update-slice_fusion.7
  61.7 10.5 %collective-permute-done.5 = bf16[512,512]{1,0:T(8,128)(2,1)S(1)} collective-permute-done((bf16[512,512]{1,0:T(8,128)(2,1)S(1)}, bf16[512,512]{1,0:T(8,128)(2,1)S(1)}, u32[]{:S(2)}, u32[]{:S(2)}) %collective-permute-start.5) | collective-permute-done | bytes 524320 | tf_op jit(solution)/shard_map/ppermute | solution.py:23
  72.2 0.8 bitcast_dynamic-update-slice_fusion.6
  73.1 0.9 bitcast_dynamic-update-slice_fusion.5
  73.9 0.8 bitcast_dynamic-update-slice_fusion.4
  74.8 9.0 %collective-permute-done.6 = bf16[512,512]{1,0:T(8,128)(2,1)S(1)} collective-permute-done((bf16[512,512]{1,0:T(8,128)(2,1)S(1)}, bf16[512,512]{1,0:T(8,128)(2,1)S(1)}, u32[]{:S(2)}, u32[]{:S(2)}) %collective-permute-start.6) | collective-permute-done | bytes 524320 | tf_op jit(solution)/shard_map/ppermute | solution.py:23
  83.7 0.8 bitcast_dynamic-update-slice_fusion.3
  84.6 0.8 bitcast_dynamic-update-slice_fusion.2
  85.4 0.8 bitcast_dynamic-update-slice_fusion.1
  86.2 8.2 %collective-permute-done.7 = bf16[512,512]{1,0:T(8,128)(2,1)S(1)} collective-permute-done((bf16[512,512]{1,0:T(8,128)(2,1)S(1)}, bf16[512,512]{1,0:T(8,128)(2,1)S(1)}, u32[]{:S(2)}, u32[]{:S(2)}) %collective-permute-start.7) | collective-permute-done | bytes 524320 | tf_op jit(solution)/shard_map/ppermute | solution.py:23
  94.5 0.8 bitcast_dynamic-update-slice_fusion
  95.3 4.9 %gather_fusion = bf16[8,512,512]{2,1,0:T(8,128)(2,1)} fusion(bf16[8,512,512]{2,1,0:T(8,128)(2,1)} %bitcast_dynamic-update-slice_fusion, s32[1024]{0:T(1024)S(1)} %pad_clamp_fusion), kind=kCustom, calls=%fused_computation | custom fusion | bytes 8388640 | tf_op jit(solution)/shard_map/gather | solution.py:25
  100.2 6.7 %collective-permute-start.8 = (bf16[4096,512]{1,0:T(8,128)(2,1)}, bf16[4096,512]{1,0:T(8,128)(2,1)}, u32[]{:S(2)}, u32[]{:S(2)}) collective-permute-start(bf16[4096,512]{1,0:T(8,128)(2,1)} %bitcast.165), channel_id=1, source_target_pairs={{0,24},{8,0},{16,8},{24,16},{1,25},{9,1},{17,9},{25,17},{2,26},{10... | collective-permute-start | bytes 12582920 | tf_op jit(solution)/shard_map/ppermute | solution.py:31
  106.9 12.8 %all-gather = s32[8,1,2]{2,1,0:T(1,128)S(1)} all-gather(s32[1,1,2]{2,1,0:T(1,128)S(1)} %bitcast.178), channel_id=1, replica_groups=mesh['src'=4,'help'=8] {'help'}, dimensions={0}, use_global_device_ids=true | all-gather | bytes 72 | tf_op jit(solution)/shard_map/all_gather | solution.py:75
  119.8 3.5 collective-permute-start
  124.0 29.6 %collective-permute-done = s32[8,2]{0,1:T(2,128)S(1)} collective-permute-done((s32[8,2]{0,1:T(2,128)S(1)}, s32[8,2]{0,1:T(2,128)S(1)}, u32[]{:S(2)}, u32[]{:S(2)}) %collective-permute-start) | collective-permute-done | bytes 96 | tf_op jit(solution)/shard_map/ppermute | solution.py:31
  153.7 3.1 multiply_reduce_fusion.1
  156.8 3.1 multiply_reduce_fusion
  160.0 13.1 %fusion.6 = (f32[512]{0:T(512)S(1)}, f32[512,8192]{0,1:T(8,128)S(1)}) fusion(pred[512]{0:T(512)(128)(4,1)S(1)} %iota_compare_fusion.6, pred[8192]{0:T(1024)(128)(4,1)S(1)} %and.99, bf16[512,512]{1,0:T(8,128)(2,1)S(1)} %copy-done.3, bf16[4096,512]{1,0:T(8,128)(2,1)} %collective-permute-done.8, bf16[4096,512]{1,0:T(8,128)(2,1)} %bitcast.166, ...), kind=kOutput, calls=%fused_computation.24 | convolution fusion | flops 4345298432 | bytes 25735680 | tf_op jit(solution)/shard_map/dot_general | solution.py:104
  173.1 7.0 %exponential_reduce_fusion.3 = f32[512]{0:T(512)S(1)} fusion(f32[512,8192]{0,1:T(8,128)S(1)} %get-tuple-element.304, f32[512]{0:T(512)S(1)} %get-tuple-element.303, pred[512]{0:T(512)(128)(4,1)S(1)} %iota_compare_fusion.6, pred[8192]{0:T(1024)(128)(4,1)S(1)} %and.99), kind=kLoop, calls=%fused_computation.23 | loop fusion | flops 25165312 | bytes 16790016 | tf_op jit(solution)/shard_map/reduce_sum | solution.py:121
  180.2 4.6 %fusion.7 = f32[8192]{0:T(1024)S(1)} fusion(f32[512,8192]{0,1:T(8,128)S(1)} %get-tuple-element.304, f32[512]{0:T(512)S(1)} %multiply_select_fusion.1, pred[512]{0:T(512)(128)(4,1)S(1)} %iota_compare_fusion.6, pred[8192]{0:T(1024)(128)(4,1)S(1)} %and.99), kind=kLoop, calls=%fused_computation.25 | loop fusion | flops 20963328 | bytes 16820736 | tf_op jit(solution)/shard_map/reduce_max | solution.py:127
  184.8 6.6 %exponential_reduce_fusion.2 = f32[8192]{0:T(1024)S(1)} fusion(f32[512,8192]{0,1:T(8,128)S(1)} %get-tuple-element.304, f32[8192]{0:T(1024)S(1)} %fusion.7, f32[512]{0:T(512)S(1)} %multiply_select_fusion.1, pred[512]{0:T(512)(128)(4,1)S(1)} %iota_compare_fusion.6, pred[8192]{0:T(1024)(128)(4,1)S(1)} %and.99), kind=kLoop, calls=%fused_computation.22 | loop fusion | flops 25157632 | bytes 16853504 | tf_op jit(solution)/shard_map/reduce_sum | solution.py:128
  191.5 24.8 %all_gather.17 = f32[8,2,8,512]{3,2,1,0:T(8,128)S(1)} all-gather(f32[1,2,8,512]{3,2,1,0:T(8,128)S(1)} %all_gather_reshape.13), channel_id=1, replica_groups=mesh['src'=4,'help'=8] {'help'}, dimensions={0}, use_global_device_ids=true | all-gather | bytes 294912 | tf_op jit(solution)/shard_map/all_gather | solution.py:35
  216.2 24.8 %all_gather.16 = f32[8,2,8,512]{3,2,1,0:T(8,128)S(1)} all-gather(f32[1,2,8,512]{3,2,1,0:T(8,128)S(1)} %all_gather_reshape.12), channel_id=1, replica_groups=mesh['src'=4,'help'=8] {'help'}, dimensions={0}, use_global_device_ids=true | all-gather | bytes 294912 | tf_op jit(solution)/shard_map/all_gather | solution.py:35
  241.1 0.4 while.34
  241.5 11.9 %collective-permute-start.9 = (f32[8,512]{1,0:T(8,128)S(1)}, f32[8,512]{1,0:T(8,128)S(1)}, u32[]{:S(2)}, u32[]{:S(2)}) collective-permute-start(f32[8,512]{1,0:T(8,128)S(1)} %slice_bitcast_fusion.7), channel_id=1, source_target_pairs={{0,8},{8,16},{16,24},{24,0},{1,9},{9,17},{17,25},{25,1},{2,10},{10... | collective-permute-start | bytes 49160 | tf_op jit(solution)/shard_map/ppermute | solution.py:31
  253.4 0.8 collective-permute-done.9
  254.6 2.4 collective-permute-start.11
  257.0 1.4 collective-permute-done.11
  258.4 10.3 %fusion.8 = f32[512]{0:T(512)S(1)} fusion(f32[512,8192]{0,1:T(8,128)} %copy-done, f32[8192]{0:T(1024)S(1)} %bitcast.168, pred[512]{0:T(512)(128)(4,1)S(1)} %iota_compare_fusion.6, pred[8192]{0:T(1024)(128)(4,1)S(1)} %and.99), kind=kLoop, calls=%fused_computation.26 | loop fusion | flops 20971008 | bytes 16820736 | tf_op jit(solution)/shard_map/reduce_max | solution.py:120
  268.7 5.6 %exponential_reduce_fusion.1 = f32[512]{0:T(512)S(1)} fusion(f32[512,8192]{0,1:T(8,128)S(1)} %copy-done.1, f32[512]{0:T(512)S(1)} %fusion.8, f32[8192]{0:T(1024)S(1)} %bitcast.169, pred[512]{0:T(512)(128)(4,1)S(1)} %iota_compare_fusion.6, pred[8192]{0:T(1024)(128)(4,1)S(1)} %and.99), kind=kLoop, calls=%fused_computation.21 | loop fusion | flops 25165312 | bytes 16822784 | tf_op jit(solution)/shard_map/reduce_sum | solution.py:121
  274.4 4.8 %fusion.9 = f32[8192]{0:T(1024)S(1)} fusion(f32[512,8192]{0,1:T(8,128)S(1)} %copy-done.1, f32[512]{0:T(512)S(1)} %multiply_select_fusion, pred[512]{0:T(512)(128)(4,1)S(1)} %iota_compare_fusion.6, pred[8192]{0:T(1024)(128)(4,1)S(1)} %and.99), kind=kLoop, calls=%fused_computation.27 | loop fusion | flops 20963328 | bytes 16820736 | tf_op jit(solution)/shard_map/reduce_max | solution.py:127
  279.2 6.7 %exponential_reduce_fusion = f32[8192]{0:T(1024)S(1)} fusion(f32[512,8192]{0,1:T(8,128)S(1)} %copy-done.1, f32[8192]{0:T(1024)S(1)} %fusion.9, f32[512]{0:T(512)S(1)} %multiply_select_fusion, pred[512]{0:T(512)(128)(4,1)S(1)} %iota_compare_fusion.6, pred[8192]{0:T(1024)(128)(4,1)S(1)} %and.99), kind=kLoop, calls=%fused_computation.20 | loop fusion | flops 25157632 | bytes 16853504 | tf_op jit(solution)/shard_map/reduce_sum | solution.py:128
  285.9 24.4 %all_gather.19 = f32[8,2,8,512]{3,2,1,0:T(8,128)S(1)} all-gather(f32[1,2,8,512]{3,2,1,0:T(8,128)S(1)} %all_gather_reshape.15), channel_id=1, replica_groups=mesh['src'=4,'help'=8] {'help'}, dimensions={0}, use_global_device_ids=true | all-gather | bytes 294912 | tf_op jit(solution)/shard_map/all_gather | solution.py:35
  310.3 24.6 %all_gather.18 = f32[8,2,8,512]{3,2,1,0:T(8,128)S(1)} all-gather(f32[1,2,8,512]{3,2,1,0:T(8,128)S(1)} %all_gather_reshape.14), channel_id=1, replica_groups=mesh['src'=4,'help'=8] {'help'}, dimensions={0}, use_global_device_ids=true | all-gather | bytes 294912 | tf_op jit(solution)/shard_map/all_gather | solution.py:35
  334.8 0.4 while.35
  335.3 12.6 %collective-permute-start.12 = (f32[8,512]{1,0:T(8,128)S(1)}, f32[8,512]{1,0:T(8,128)S(1)}, u32[]{:S(2)}, u32[]{:S(2)}) collective-permute-start(f32[8,512]{1,0:T(8,128)S(1)} %slice_bitcast_fusion.5), channel_id=1, source_target_pairs={{0,8},{8,16},{16,24},{24,0},{1,9},{9,17},{17,25},{25,1},{2,10},{10... | collective-permute-start | bytes 49160 | tf_op jit(solution)/shard_map/ppermute | solution.py:31
  348.0 0.8 collective-permute-done.12
  349.1 2.1 collective-permute-start.14
  351.3 0.6 constant_dynamic-slice_fusion
  351.9 0.9 collective-permute-done.14
  352.8 8.1 %convert_reduce_fusion = (f32[512]{0:T(512)S(1)}, bf16[512,8192]{0,1:T(8,128)(2,1)S(1)}) fusion(f32[512,8192]{0,1:T(8,128)} %copy-done, f32[8192]{0:T(1024)S(1)} %bitcast.170, f32[512]{0:T(512)S(1)} %multiply_select_fusion, pred[8192]{0:T(1024)(128)(4,1)S(1)} %and.99, pred[512]{0:T(512)(128)(4,1)S(1)} %iota_compare_fusion.6), kind=kLoop, calls=%fused_computation.19 | loop fusion | flops 33553920 | bytes 25211392 | tf_op jit(solution)/shard_map/reduce_sum | solution.py:144
  360.9 7.7 %fusion.12 = f32[512,512]{1,0:T(8,128)} fusion(bf16[512,8192]{0,1:T(8,128)(2,1)S(1)} %get-tuple-element.298, bf16[4096,512]{1,0:T(8,128)(2,1)} %collective-permute-done.8, bf16[4096,512]{1,0:T(8,128)(2,1)S(1)} %bitcast.167, f32[512]{0:T(512)S(1)} %broadcast_select_fusion, pred[512]{0:T(512)(128)(4,1)S(1)} %iota_compare_fusion.6), kind=kOutput, calls=%fused_computation.33 | convolution fusion | flops 4312268800 | bytes 17828352 | tf_op jit(solution)/shard_map/dot_general | solution.py:143
  (88 shorter events, 2.5 us)
Async XLA Ops:
  0.6 106.3 %copy-start.5 = (s32[1,2]{1,0:T(1,128)S(1)}, s32[1,2]{1,0:T(1,128)}, u32[]{:S(2)}) copy-start(s32[1,2]{1,0:T(1,128)} %param.11) | copy-start | bytes 28
  0.6 122.7 %copy-start.6 = (s32[2,64]{1,0:T(2,128)S(1)}, s32[2,64]{1,0:T(2,128)}, u32[]{:S(2)}) copy-start(s32[2,64]{1,0:T(2,128)} %param.9) | copy-start | bytes 1540
  0.7 122.7 %copy-start.7 = (s32[2,32]{1,0:T(2,128)S(1)}, s32[2,32]{1,0:T(2,128)}, u32[]{:S(2)}) copy-start(s32[2,32]{1,0:T(2,128)} %param.10) | copy-start | bytes 772
  0.7 122.9 %copy-start.3 = (bf16[512,512]{1,0:T(8,128)(2,1)S(1)}, bf16[512,512]{1,0:T(8,128)(2,1)}, u32[]{:S(2)}) copy-start(bf16[512,512]{1,0:T(8,128)(2,1)} %param.12) | copy-start | bytes 1572868
  0.7 17.0 %collective-permute-start.1 = (bf16[512,512]{1,0:T(8,128)(2,1)}, bf16[512,512]{1,0:T(8,128)(2,1)S(1)}, u32[]{:S(2)}, u32[]{:S(2)}) collective-permute-start(bf16[512,512]{1,0:T(8,128)(2,1)} %param.13), channel_id=1, source_target_pairs={{0,1},{1,2},{2,3},{3,4},{4,5},{5,6},{6,7},{7,0},{8,9},{9,10},{10,1... | collective-permute-start | bytes 1572872 | tf_op jit(solution)/shard_map/ppermute | solution.py:23
  17.6 14.9 %collective-permute-start.2 = (bf16[512,512]{1,0:T(8,128)(2,1)S(1)}, bf16[512,512]{1,0:T(8,128)(2,1)S(1)}, u32[]{:S(2)}, u32[]{:S(2)}) collective-permute-start(bf16[512,512]{1,0:T(8,128)(2,1)S(1)} %collective-permute-done.1), channel_id=1, source_target_pairs={{0,1},{1,2},{2,3},{3,4},{4,5},{5,6},{6,7},{7,0},{8,9},{9,10},{10,1... | collective-permute-start | bytes 1572872 | tf_op jit(solution)/shard_map/ppermute | solution.py:23
  32.6 14.1 %collective-permute-start.3 = (bf16[512,512]{1,0:T(8,128)(2,1)S(1)}, bf16[512,512]{1,0:T(8,128)(2,1)S(1)}, u32[]{:S(2)}, u32[]{:S(2)}) collective-permute-start(bf16[512,512]{1,0:T(8,128)(2,1)S(1)} %collective-permute-done.2), channel_id=1, source_target_pairs={{0,1},{1,2},{2,3},{3,4},{4,5},{5,6},{6,7},{7,0},{8,9},{9,10},{10,1... | collective-permute-start | bytes 1572872 | tf_op jit(solution)/shard_map/ppermute | solution.py:23
  46.6 13.2 %collective-permute-start.4 = (bf16[512,512]{1,0:T(8,128)(2,1)S(1)}, bf16[512,512]{1,0:T(8,128)(2,1)S(1)}, u32[]{:S(2)}, u32[]{:S(2)}) collective-permute-start(bf16[512,512]{1,0:T(8,128)(2,1)S(1)} %collective-permute-done.3), channel_id=1, source_target_pairs={{0,1},{1,2},{2,3},{3,4},{4,5},{5,6},{6,7},{7,0},{8,9},{9,10},{10,1... | collective-permute-start | bytes 1572872 | tf_op jit(solution)/shard_map/ppermute | solution.py:23
  59.9 12.4 %collective-permute-start.5 = (bf16[512,512]{1,0:T(8,128)(2,1)S(1)}, bf16[512,512]{1,0:T(8,128)(2,1)S(1)}, u32[]{:S(2)}, u32[]{:S(2)}) collective-permute-start(bf16[512,512]{1,0:T(8,128)(2,1)S(1)} %collective-permute-done.4), channel_id=1, source_target_pairs={{0,1},{1,2},{2,3},{3,4},{4,5},{5,6},{6,7},{7,0},{8,9},{9,10},{10,1... | collective-permute-start | bytes 1572872 | tf_op jit(solution)/shard_map/ppermute | solution.py:23
  72.2 11.5 %collective-permute-start.6 = (bf16[512,512]{1,0:T(8,128)(2,1)S(1)}, bf16[512,512]{1,0:T(8,128)(2,1)S(1)}, u32[]{:S(2)}, u32[]{:S(2)}) collective-permute-start(bf16[512,512]{1,0:T(8,128)(2,1)S(1)} %collective-permute-done.5), channel_id=1, source_target_pairs={{0,1},{1,2},{2,3},{3,4},{4,5},{5,6},{6,7},{7,0},{8,9},{9,10},{10,1... | collective-permute-start | bytes 1572872 | tf_op jit(solution)/shard_map/ppermute | solution.py:23
  83.7 10.7 %collective-permute-start.7 = (bf16[512,512]{1,0:T(8,128)(2,1)S(1)}, bf16[512,512]{1,0:T(8,128)(2,1)S(1)}, u32[]{:S(2)}, u32[]{:S(2)}) collective-permute-start(bf16[512,512]{1,0:T(8,128)(2,1)S(1)} %collective-permute-done.6), channel_id=1, source_target_pairs={{0,1},{1,2},{2,3},{3,4},{4,5},{5,6},{6,7},{7,0},{8,9},{9,10},{10,1... | collective-permute-start | bytes 1572872 | tf_op jit(solution)/shard_map/ppermute | solution.py:23
  100.2 56.6 %collective-permute-start.8 = (bf16[4096,512]{1,0:T(8,128)(2,1)}, bf16[4096,512]{1,0:T(8,128)(2,1)}, u32[]{:S(2)}, u32[]{:S(2)}) collective-permute-start(bf16[4096,512]{1,0:T(8,128)(2,1)} %bitcast.165), channel_id=1, source_target_pairs={{0,24},{8,0},{16,8},{24,16},{1,25},{9,1},{17,9},{25,17},{2,26},{10... | collective-permute-start | bytes 12582920 | tf_op jit(solution)/shard_map/ppermute | solution.py:31
  119.8 33.8 %collective-permute-start = (s32[8,2]{0,1:T(2,128)S(1)}, s32[8,2]{0,1:T(2,128)S(1)}, u32[]{:S(2)}, u32[]{:S(2)}) collective-permute-start(s32[8,2]{0,1:T(2,128)S(1)} %bitcast.184), channel_id=1, source_target_pairs={{0,24},{8,0},{16,8},{24,16},{1,25},{9,1},{17,9},{25,17},{2,26},{10... | collective-permute-start | bytes 200 | tf_op jit(solution)/shard_map/ppermute | solution.py:31
  173.1 11.7 %copy-start = (f32[512,8192]{0,1:T(8,128)}, f32[512,8192]{0,1:T(8,128)S(1)}, u32[]{:S(2)}) copy-start(f32[512,8192]{0,1:T(8,128)S(1)} %get-tuple-element.304) | copy-start | bytes 50331652
  241.5 12.7 %collective-permute-start.9 = (f32[8,512]{1,0:T(8,128)S(1)}, f32[8,512]{1,0:T(8,128)S(1)}, u32[]{:S(2)}, u32[]{:S(2)}) collective-permute-start(f32[8,512]{1,0:T(8,128)S(1)} %slice_bitcast_fusion.7), channel_id=1, source_target_pairs={{0,8},{8,16},{16,24},{24,0},{1,9},{9,17},{17,25},{25,1},{2,10},{10... | collective-permute-start | bytes 49160 | tf_op jit(solution)/shard_map/ppermute | solution.py:31
  253.3 1.2 collective-permute-start.10
  254.6 3.8 %collective-permute-start.11 = (f32[8,512]{1,0:T(8,128)S(1)}, f32[8,512]{1,0:T(8,128)S(1)}, u32[]{:S(2)}, u32[]{:S(2)}) collective-permute-start(f32[8,512]{1,0:T(8,128)S(1)} %fusion.26), channel_id=1, source_target_pairs={{0,24},{8,0},{16,8},{24,16},{1,25},{9,1},{17,9},{25,17},{2,26},{10... | collective-permute-start | bytes 49160 | tf_op jit(solution)/shard_map/ppermute | solution.py:31
  257.0 11.7 %copy-start.1 = (f32[512,8192]{0,1:T(8,128)S(1)}, f32[512,8192]{0,1:T(8,128)}, u32[]{:S(2)}) copy-start(f32[512,8192]{0,1:T(8,128)} %copy-done) | copy-start | bytes 50331652
  274.3 78.4 %copy-start.4 = (f32[512]{0:T(512)}, f32[512]{0:T(512)S(1)}, u32[]{:S(2)}) copy-start(f32[512]{0:T(512)S(1)} %multiply_select_fusion) | copy-start | bytes 6148
  335.3 13.5 %collective-permute-start.12 = (f32[8,512]{1,0:T(8,128)S(1)}, f32[8,512]{1,0:T(8,128)S(1)}, u32[]{:S(2)}, u32[]{:S(2)}) collective-permute-start(f32[8,512]{1,0:T(8,128)S(1)} %slice_bitcast_fusion.5), channel_id=1, source_target_pairs={{0,8},{8,16},{16,24},{24,0},{1,9},{9,17},{17,25},{25,1},{2,10},{10... | collective-permute-start | bytes 49160 | tf_op jit(solution)/shard_map/ppermute | solution.py:31
  347.9 1.2 collective-permute-start.13
  348.0 13.0 %copy-start.2 = (bf16[8,512,512]{2,1,0:T(8,128)(2,1)S(1)}, bf16[8,512,512]{2,1,0:T(8,128)(2,1)}, u32[]{:S(2)}) copy-start(bf16[8,512,512]{2,1,0:T(8,128)(2,1)} %gather_fusion) | copy-start | bytes 12582916
  349.1 3.6 collective-permute-start.14
